TPU v7x, 32 devices: a whole 2x2x4 slice. The times are simulated.
32 devices in a mesh: dp: 8 (over z, x), mp: 4 (over y, core).
Axes of the slice: x: 2, y: 2, z: 4, core: 2. Of those that a mesh axis runs over, the one named last changes fastest.
Arguments:
- block_in: bfloat16 [8, 2048, 1024], P('dp', 'mp'), may hold values from -6 to 6
- segment_ids: int32 [8, 2048], P('dp', 'mp'), may hold values from 0 to 15, never falling along the last dimension, each value on 1 to 1024 neighbouring positions
- first_gain: bfloat16 [1024], P(('dp', 'mp')), may hold values from 0.5 to 1.5
- in_proj: bfloat16 [1024, 3072], P(('dp', 'mp')), may hold values from -0.1875 to 0.1875
- conv_kernel: bfloat16 [1024, 3], P(('dp', 'mp')), may hold values from -3 to 3
- out_proj: bfloat16 [1024, 1024], P(('dp', 'mp')), may hold values from -0.1875 to 0.1875
- second_gain: bfloat16 [1024], P(('dp', 'mp')), may hold values from 0.5 to 1.5
- gate_proj: bfloat16 [1024, 4608], P(None, 'mp'), may hold values from -0.1875 to 0.1875
- up_proj: bfloat16 [1024, 4608], P(None, 'mp'), may hold values from -0.1875 to 0.1875
- down_proj: bfloat16 [4608, 1024], P('mp'), may hold values from -0.125 to 0.125
- out_grad: bfloat16 [8, 2048, 1024], P('dp', 'mp'), may hold values from -6 to 6
Outputs:
- layer_out: bfloat16 [8, 2048, 1024], P('dp', 'mp')
- input_grad: float32 [8, 2048, 1024], P('dp', 'mp')
- grad_first: float32 [1024], P(('dp', 'mp'))
- grad_in: float32 [1024, 3072], P(('dp', 'mp'))
- grad_conv: float32 [1024, 3], P(('dp', 'mp'))
- grad_out: float32 [1024, 1024], P(('dp', 'mp'))
- grad_second: float32 [1024], P(('dp', 'mp'))
- grad_gate: float32 [1024, 4608], P(None, 'mp')
- grad_up: float32 [1024, 4608], P(None, 'mp')
- grad_down: float32 [4608, 1024], P('mp')
Inputs may be any that keep to these rules, and one draw needn't show every extreme that they name: `segment_ids`: along each sequence the ids never fall and each document is one run of positions; the longest document has exactly 1024 tokens.
All inputs are finite; a program needn't handle non-finite values.
Results may differ from a plain program's by a relative error of at most 0.013.
Values may be sent and summed in bfloat16 or wider, within the bound.
No kernel may reach another device: no remote copies, remote signals or barrier semaphores. Data moves between devices by JAX's collectives and lax.ppermute only.
A program may use at most 192 MiB of HBM per device.

v0:
```python
import jax
import jax.numpy as jnp
from jax import lax
from jax.sharding import PartitionSpec as P

KERNEL = 3
epsilon = 1e-05


def from_behind(block, axis, distance):
    devices = range(lax.axis_size(axis))
    route = [(i - distance, i) for i in devices if i - distance in devices]
    return lax.ppermute(block, axis, route)


def rms_norm(values, scale):
    return values * lax.rsqrt(jnp.mean(values * values, axis=-1, keepdims=True) + epsilon) * scale


def swiglu(gate_val, up_val):
    return jax.nn.silu(gate_val) * up_val


def inner_rows(left, right):
    return lax.dot_general(
        left, right, (((0,), (0,)), ((), ())), preferred_element_type=jnp.float32
    )


def inner_cols(left, right):
    return lax.dot_general(
        left, right, (((1,), (1,)), ((), ())), preferred_element_type=jnp.float32
    )


def causal_conv(product, rim_rows, own_ids, rim_ids, kernel):
    length = product.shape[0]
    extended = jnp.concatenate([rim_rows, product], 0)
    extended_ids = jnp.concatenate([rim_ids, own_ids], 0)
    summed = jnp.zeros_like(product)
    for offset in range(KERNEL):
        same = (extended_ids[offset : offset + length] == own_ids)[:, None]
        summed = (
            summed + jnp.where(same, extended[offset : offset + length], 0.0) * kernel[:, offset]
        )
    return summed


def per_device(
    block_in,
    segment_ids,
    first_gain,
    in_proj,
    conv_kernel,
    out_proj,
    second_gain,
    gate_proj,
    up_proj,
    down_proj,
    out_grad,
):
    row_count = block_in.shape[1]
    features = block_in.shape[2]
    lookback = KERNEL - 1
    residual_in = block_in.reshape(row_count, features).astype(jnp.float32)
    own_ids = segment_ids.reshape(row_count).astype(jnp.float32)
    gain_one, weight_in, kernel_all, weight_out, gain_two = (
        lax.all_gather(first_gain, ("dp", "mp"), axis=0, tiled=True),
        lax.all_gather(in_proj, ("dp", "mp"), axis=0, tiled=True),
        lax.all_gather(conv_kernel, ("dp", "mp"), axis=0, tiled=True),
        lax.all_gather(out_proj, ("dp", "mp"), axis=0, tiled=True),
        lax.all_gather(second_gain, ("dp", "mp"), axis=0, tiled=True),
    )
    first_normed, first_pull = jax.vjp(rms_norm, residual_in, gain_one.astype(jnp.float32))
    first_low = first_normed.astype(jnp.bfloat16)
    mixer = jnp.dot(first_low, weight_in, preferred_element_type=jnp.float32)
    opening = mixer[:, :features]
    closing = mixer[:, features : 2 * features]
    carried = mixer[:, 2 * features :]
    product = opening * carried
    rim_rows, rim_ids = from_behind(
        (product[row_count - lookback :], own_ids[row_count - lookback :]), "mp", 1
    )

    def gated_conv(product_in, closing_in, rim_in, kernel_in):
        return closing_in * causal_conv(product_in, rim_in, own_ids, rim_ids, kernel_in)

    gated, conv_pull = jax.vjp(
        gated_conv, product, closing, rim_rows, kernel_all.astype(jnp.float32)
    )
    gated_low = gated.astype(jnp.bfloat16)
    residual = residual_in + jnp.dot(gated_low, weight_out, preferred_element_type=jnp.float32)
    second_normed, second_pull = jax.vjp(rms_norm, residual, gain_two.astype(jnp.float32))
    second_low = second_normed.astype(jnp.bfloat16)
    group_rows = lax.all_gather(second_low, "mp", axis=0, tiled=True)
    gate_val = jnp.dot(group_rows, gate_proj, preferred_element_type=jnp.float32)
    up_val = jnp.dot(group_rows, up_proj, preferred_element_type=jnp.float32)
    activated, swiglu_pull = jax.vjp(swiglu, gate_val, up_val)
    hidden = activated.astype(jnp.bfloat16)
    offset_rows = lax.axis_index("mp") * row_count
    branch_sums = lax.psum(
        jnp.dot(hidden, down_proj, preferred_element_type=jnp.float32).astype(jnp.bfloat16), "mp"
    ).astype(jnp.float32)
    branch_out = lax.dynamic_slice_in_dim(branch_sums, offset_rows, row_count, 0)
    layer_out = (residual + branch_out).astype(jnp.bfloat16).reshape(1, row_count, features)
    cotangent = out_grad.reshape(row_count, features)
    cotangent_group = lax.all_gather(cotangent, "mp", axis=0, tiled=True)
    down_local = inner_rows(hidden, cotangent_group)
    hidden_grad = inner_cols(cotangent_group, down_proj)
    gate_grad, up_grad = swiglu_pull(hidden_grad)
    gate_low = gate_grad.astype(jnp.bfloat16)
    up_low = up_grad.astype(jnp.bfloat16)
    gate_local = inner_rows(group_rows, gate_low)
    up_local = inner_rows(group_rows, up_low)
    backward_sums = lax.psum(
        (inner_cols(gate_low, gate_proj) + inner_cols(up_low, up_proj)).astype(jnp.bfloat16), "mp"
    ).astype(jnp.float32)
    normed_grad = lax.dynamic_slice_in_dim(backward_sums, offset_rows, row_count, 0)
    residual_part, second_local = second_pull(normed_grad)
    residual_grad = cotangent.astype(jnp.float32) + residual_part
    residual_low = residual_grad.astype(jnp.bfloat16)
    out_local = inner_rows(gated_low, residual_low)
    gated_grad = inner_cols(residual_low, weight_out)
    product_grad, closing_grad, rim_grad, kernel_local = conv_pull(gated_grad)
    rim_back = from_behind(rim_grad, "mp", -1)
    product_grad = product_grad + jnp.pad(rim_back, ((row_count - lookback, 0), (0, 0)))
    mixer_grad = jnp.concatenate(
        [product_grad * carried, closing_grad, product_grad * opening], 1
    ).astype(jnp.bfloat16)
    in_local = inner_rows(first_low, mixer_grad)
    first_grad = inner_cols(mixer_grad, weight_in)
    input_part, first_local = first_pull(first_grad)
    input_grad = (residual_grad + input_part).reshape(1, row_count, features)
    grad_gate, grad_up, grad_down = (
        lax.psum(gate_local.astype(jnp.bfloat16), "dp").astype(jnp.float32),
        lax.psum(up_local.astype(jnp.bfloat16), "dp").astype(jnp.float32),
        lax.psum(down_local.astype(jnp.bfloat16), "dp").astype(jnp.float32),
    )
    grad_first, grad_in, grad_conv, grad_out, grad_second = (
        lax.psum_scatter(first_local, ("dp", "mp"), scatter_dimension=0, tiled=True),
        lax.psum_scatter(in_local, ("dp", "mp"), scatter_dimension=0, tiled=True),
        lax.psum_scatter(kernel_local, ("dp", "mp"), scatter_dimension=0, tiled=True),
        lax.psum_scatter(out_local, ("dp", "mp"), scatter_dimension=0, tiled=True),
        lax.psum_scatter(second_local, ("dp", "mp"), scatter_dimension=0, tiled=True),
    )
    return (
        layer_out,
        input_grad,
        grad_first,
        grad_in,
        grad_conv,
        grad_out,
        grad_second,
        grad_gate,
        grad_up,
        grad_down,
    )


def solution(mesh):
    in_specs = (
        P("dp", "mp", None),
        P("dp", "mp"),
        P(("dp", "mp")),
        P(("dp", "mp"), None),
        P(("dp", "mp"), None),
        P(("dp", "mp"), None),
        P(("dp", "mp")),
        P(None, "mp"),
        P(None, "mp"),
        P("mp", None),
        P("dp", "mp", None),
    )
    out_specs = (
        P("dp", "mp", None),
        P("dp", "mp", None),
        P(("dp", "mp")),
        P(("dp", "mp"), None),
        P(("dp", "mp"), None),
        P(("dp", "mp"), None),
        P(("dp", "mp")),
        P(None, "mp"),
        P(None, "mp"),
        P("mp", None),
    )
    return jax.shard_map(
        per_device, mesh=mesh, in_specs=in_specs, out_specs=out_specs, check_vma=False
    )
```

profile of v0, /device:TPU:0, one launch (start us, length us, event | category | flops | bytes accessed | tf_op | source)
XLA Modules:
  0.0 1103.1 jit_solution(15660055661368846921)
XLA Ops:
  7.2 0.7 all-gather.7.cloned.1.call-update
  8.0 0.7 all-gather.9.cloned.1.call-update
  8.7 0.7 convert_element_type.89
  9.5 2.3 collective-permute-start
  11.9 0.8 dynamic-update-slice
  12.7 0.8 dynamic-update-slice.1
  13.5 41.9 %all-reduce.12 = (bf16[1024]{0:T(1024)(128)(2,1)S(1)}, bf16[1024]{0:T(1024)(128)(2,1)S(1)}) all-reduce(bf16[1024]{0:T(1024)(128)(2,1)S(1)} %dynamic-update-slice, bf16[1024]{0:T(1024)(128)(2,1)S(1)} %dynamic-update-slice.1), channel_id=1, replica_groups=mesh['dp'=8,'mp'=4] {'dp','mp'}, use_global_device_ids=true, to_apply=%add.7 | all-reduce | flops 2048 | bytes 8192
  55.4 40.8 %all-gather.1 = bf16[32,32,3]{1,2,0:T(4,128)(2,1)S(1)} all-gather(bf16[1,32,3]{1,2,0:T(4,128)(2,1)} %bitcast.74), channel_id=1, replica_groups=mesh['dp'=8,'mp'=4] {'dp','mp'}, dimensions={0}, use_global_device_ids=true | all-gather | bytes 6336 | tf_op jit(solution)/shard_map/all_gather | solution.py:70
  96.2 0.1 reshape.110
  96.3 1.5 fusion.24
  98.0 6.0 fusion.35
  104.0 0.4 slice_multiply_fusion
  104.4 2.2 collective-permute-start.1
  106.7 0.7 collective-permute-done.1
  107.4 2.5 multiply_convert_fusion.6
  110.0 31.3 %all-gather.9.cloned.1.call-done = bf16[1024,1024]{1,0:T(8,128)(2,1)} async-done(((bf16[32,1024]{1,0:T(8,128)(2,1)}), bf16[1024,1024]{1,0:T(8,128)(2,1)}) %all-gather.9.cloned.1.call-update) | async-done | bytes 2097168 | tf_op jit(solution)/shard_map/all_gather | solution.py:71
  141.3 3.3 multiply_reduce_fusion.3
  144.6 1.4 copy-done.7
  146.0 1.2 multiply_convert_fusion.5
  147.2 0.5 all-gather.13.cloned.1.call-update
  147.8 0.6 all-reduce.20.cloned.1.call-start
  148.3 32.3 %all-gather.11.cloned.1.call-done = bf16[2048,1024]{1,0:T(8,128)(2,1)} async-done(((bf16[512,1024]{1,0:T(8,128)(2,1)}), bf16[2048,1024]{1,0:T(8,128)(2,1)}) %all-gather.11.cloned.1.call-update) | async-done | bytes 4194320 | tf_op jit(solution)/shard_map/all_gather | solution.py:95
  180.7 10.6 fusion.42
  191.3 7.9 fusion.43
  199.2 17.5 %all-gather.13.cloned.1.call-done = bf16[1,2048,1024]{2,1,0:T(8,128)(2,1)} async-done(((bf16[1,512,1024]{2,1,0:T(8,128)(2,1)}), bf16[1,2048,1024]{2,1,0:T(8,128)(2,1)}) %all-gather.13.cloned.1.call-update) | async-done | bytes 4194320 | tf_op jit(solution)/shard_map/all_gather | solution.py:107
  216.6 18.2 %multiply_convert_fusion = (bf16[2048,1152]{1,0:T(8,128)(2,1)}, bf16[2048,1152]{1,0:T(8,128)(2,1)}, bf16[2048,1152]{1,0:T(8,128)(2,1)}) fusion(f32[2048,1152]{1,0:T(8,128)} %fusion.42, f32[2048,1152]{1,0:T(8,128)} %fusion.43, bf16[1152,1024]{1,0:T(8,128)(2,1)S(1)} %copy-done, bf16[1,2048,1024]{2,1,0:T(8,128)(2,1)} %all-gather.13.cloned.1.call-done), kind=kOutput, calls=%fused_computation.4 | convolution fusion | flops 4869586944 | bytes 39583744 | tf_op jit(solution)/shard_map/dot_general | solution.py:31
  234.9 7.7 fusion.44
  242.6 7.1 convolution_convert_fusion.2
  249.7 7.7 add_convert_fusion
  257.5 10.1 convolution_convert_fusion
  267.6 9.6 convolution_convert_fusion.1
  277.2 133.6 %all-reduce.20.cloned.1.call-done = (bf16[2048,1024]{1,0:T(8,128)(2,1)}, bf16[2048,1024]{1,0:T(8,128)(2,1)}) async-done(((bf16[2048,1024]{1,0:T(8,128)(2,1)}, bf16[2048,1024]{1,0:T(8,128)(2,1)}), (bf16[2048,1024]{1,0:T(8,128)(2,1)}, bf16[2048,1024]{1,0:T(8,128)(2,1)})) %all-reduce.20.cloned.1.call-update) | async-done | bytes 8388624 | tf_op jit(solution)/shard_map/psum | solution.py:101
  410.8 2.0 fusion.20
  412.9 3.4 fusion.21
  416.3 1.3 fusion.32
  417.6 1.0 copy-done.4
  418.6 0.6 copy-done.10
  419.3 3.7 multiply_reduce_fusion.1
  423.0 1.1 copy.24
  424.1 9.5 fusion.8
  433.7 1.5 copy-done.6
  435.2 4.5 fusion.30
  439.8 2.0 multiply_select_fusion.2
  441.8 1.6 collective-permute-start.2
  443.4 1.0 pad_add_fusion
  444.4 0.8 collective-permute-done.2
  445.2 0.8 multiply_convert_fusion.4
  446.0 1.0 copy-done.12
  447.0 0.3 copy-done.13
  447.3 6.8 fusion.27
  454.2 8.8 fusion.18
  463.0 40.7 %all-reduce.11 = (f32[1024]{0:T(1024)S(1)}, f32[1024]{0:T(1024)S(1)}) all-reduce(f32[1024]{0:T(1024)S(1)} %get-tuple-element.15, f32[1024]{0:T(1024)S(1)} %get-tuple-element.10), channel_id=3, replica_groups=mesh['dp'=8,'mp'=4] {'dp','mp'}, use_global_device_ids=true, to_apply=%region_7.8.clone | all-reduce | flops 2048 | bytes 16384
  503.7 0.6 dynamic-slice
  504.3 0.6 dynamic-slice.1
  504.9 3.4 fusion.23
  508.4 50.0 %reduce-scatter.10.cloned.1.call-done = f32[32,3]{1,0:T(8,128)} async-done(((f32[1024,3]{1,0:T(8,128)}), f32[32,3]{1,0:T(8,128)}) %reduce-scatter.10.cloned.1.call-update) | async-done | bytes 400
  558.4 1.4 copy.25
  559.8 235.4 %all-reduce.18.cloned.1.call-done = (bf16[1024,1152]{1,0:T(8,128)(2,1)}, bf16[1024,1152]{1,0:T(8,128)(2,1)}, bf16[1152,1024]{1,0:T(8,128)(2,1)}) async-done(((bf16[1024,1152]{1,0:T(8,128)(2,1)}, bf16[1024,1152]{1,0:T(8,128)(2,1)}, bf16[1152,1024]{1,0:T(8,128)(2,1)}), (bf16[1024,1152]{1,0:T(8,128)(2,1)}, bf16[1024,1152]{1,0:T(8,128)(2,1)}, bf16[1152,1024]{1,0:T(8,128)(2,1)})) %all-reduce.18.cloned.1.call-update) | async-done | bytes 7077904 | tf_op jit(solution)/shard_map/psum | solution.py:135
  795.2 4.3 convert_element_type.106
  799.5 2.5 convert_element_type.108
  802.0 0.1 copy-done.15
  802.1 2.7 convert_element_type.110
  804.8 133.5 %reduce-scatter.8.cloned.1.call-done = f32[32,1024]{1,0:T(8,128)} async-done(((f32[1024,1024]{1,0:T(8,128)}), f32[32,1024]{1,0:T(8,128)}) %reduce-scatter.8.cloned.1.call-update) | async-done | bytes 131088 | tf_op jit(solution)/shard_map/reduce_scatter | solution.py:143
  938.4 157.9 %reduce-scatter.6.cloned.1.call-done = f32[32,3072]{1,0:T(8,128)} async-done(((f32[1024,3072]{1,0:T(8,128)}), f32[32,3072]{1,0:T(8,128)}) %reduce-scatter.6.cloned.1.call-update) | async-done | bytes 393232 | tf_op jit(solution)/shard_map/reduce_scatter | solution.py:141
  (83 shorter events, 0.9 us)
Async XLA Ops:
  7.2 209.4 %copy-start = (bf16[1152,1024]{1,0:T(8,128)(2,1)S(1)}, bf16[1152,1024]{1,0:T(8,128)(2,1)}, u32[]{:S(2)}) copy-start(bf16[1152,1024]{1,0:T(8,128)(2,1)} %param.20) | copy-start | bytes 7077892
  7.2 90.8 %all-gather.7.cloned.1.call-start = ((), (), s32[]{:S(2)}) async-start(), calls=%async_computation.3 | async-start | bytes 6488064 | tf_op jit(solution)/shard_map/all_gather | solution.py:69
  7.9 133.4 %all-gather.9.cloned.1.call-start = ((), (), s32[]{:S(2)}) async-start(), calls=%async_computation.4 | async-start | bytes 2162688 | tf_op jit(solution)/shard_map/all_gather | solution.py:71
  8.7 172.0 %all-gather.11.cloned.1.call-start = ((), (), s32[]{:S(2)}) async-start(), calls=%async_computation.5 | async-start | bytes 5242880 | tf_op jit(solution)/shard_map/all_gather | solution.py:95
  9.5 88.4 %collective-permute-start = (f32[2]{0:T(128)S(1)}, f32[2]{0:T(128)S(1)}, u32[]{:S(2)}, u32[]{:S(2)}) collective-permute-start(f32[2]{0:T(128)S(1)} %slice_bitcast_fusion), channel_id=1, source_target_pairs={{0,1},{1,2},{2,3},{4,5},{5,6},{6,7},{8,9},{9,10},{10,11},{12,13},{... | collective-permute-start | bytes 32 | tf_op jit(solution)/shard_map/ppermute | solution.py:13
  104.0 3.5 copy-start.2
  104.4 3.1 copy-start.3
  104.4 3.0 collective-permute-start.1
  107.4 33.9 %copy-start.9 = (bf16[1,512,1024]{2,1,0:T(8,128)(2,1)S(1)}, bf16[1,512,1024]{2,1,0:T(8,128)(2,1)}, u32[]{:S(2)}) copy-start(bf16[1,512,1024]{2,1,0:T(8,128)(2,1)} %param.11) | copy-start | bytes 3145732
  144.6 1.4 copy-start.7
  147.2 69.4 %all-gather.13.cloned.1.call-start = ((), (), s32[]{:S(2)}) async-start(), calls=%async_computation.8 | async-start | bytes 5242880 | tf_op jit(solution)/shard_map/all_gather | solution.py:107
  147.8 263.1 %all-reduce.20.cloned.1.call-start = ((), (), s32[]{:S(2)}) async-start(), calls=%async_computation.11 | async-start | bytes 16777216 | tf_op jit(solution)/shard_map/psum | solution.py:101
  180.7 10.6 copy-start.17
  180.7 10.6 copy-start.20
  216.6 18.2 %copy-start.19 = (bf16[1024,1152]{1,0:T(8,128)(2,1)S(1)}, bf16[1024,1152]{1,0:T(8,128)(2,1)}, u32[]{:S(2)}) copy-start(bf16[1024,1152]{1,0:T(8,128)(2,1)} %param.18) | copy-start | bytes 7077892
  234.9 7.7 copy-start.23
  234.9 14.8 %slice-start.2 = ((s8[4718592]{0:T(1024)(128)(4,1)}), s8[4194304]{0:T(1024)(128)(4,1)S(1)}, s32[]{:S(2)}) async-start(s8[4718592]{0:T(1024)(128)(4,1)} %bitcast.75), calls=%async_computation.14 | async-start | bytes 8388608
  242.5 7.2 slice-start.3
  242.6 7.1 copy-start.21
  257.5 300.9 %reduce-scatter.10.cloned.1.call-start = ((), (), s32[]{:S(2)}) async-start(), calls=%async_computation.9 | async-start | bytes 540672
  257.5 10.1 copy-start.18
  267.6 143.3 %copy-start.8 = (f32[512,1024]{1,0:T(8,128)S(1)}, f32[512,1024]{1,0:T(8,128)}, u32[]{:S(2)}) copy-start(f32[512,1024]{1,0:T(8,128)} %copy-done.7) | copy-start | bytes 6291460
  410.8 2.0 copy-start.14
  412.9 3.4 copy-start.22
  416.3 1.3 copy-start.5
  416.3 2.3 copy-start.4
  416.3 3.0 copy-start.10
  424.1 371.1 %all-reduce.18.cloned.1.call-start = ((), (), s32[]{:S(2)}) async-start(), calls=%async_computation.10 | async-start | bytes 14155776 | tf_op jit(solution)/shard_map/psum | solution.py:135
  433.6 1.6 copy-start.6
  433.7 504.7 %reduce-scatter.8.cloned.1.call-start = ((), (), s32[]{:S(2)}) async-start(), calls=%async_computation.7 | async-start | bytes 4325376 | tf_op jit(solution)/shard_map/reduce_scatter | solution.py:143
  439.7 656.6 %reduce-scatter.6.cloned.1.call-start = ((), (), s32[]{:S(2)}) async-start(), calls=%async_computation.6 | async-start | bytes 12976128 | tf_op jit(solution)/shard_map/reduce_scatter | solution.py:141
  441.8 3.4 slice-start
  441.8 3.3 slice-start.1
  441.8 3.3 collective-permute-start.2
  444.4 3.0 copy-start.11
  446.0 1.0 copy-start.12
  446.0 1.3 copy-start.13
  795.2 4.3 copy-start.16
  799.5 2.6 copy-start.15
  802.0 294.3 %copy-start.1 = (bf16[1152,1024]{1,0:T(8,128)(2,1)S(1)}, bf16[1152,1024]{1,0:T(8,128)(2,1)}, u32[]{:S(2)}) copy-start(bf16[1152,1024]{1,0:T(8,128)(2,1)} %param.20) | copy-start | bytes 7077892
Sparse Core Ops, SparseCore 0:
  10.9 72.5 all-gather.6
  86.4 54.8 all-gather.8
  147.3 33.3 all-gather.10
  182.1 34.4 all-gather.12
  257.6 153.2 all-reduce.19
  424.2 134.1 reduce-scatter.9
  563.9 231.2 all-reduce.17
  798.0 140.2 reduce-scatter.7
  945.0 151.2 reduce-scatter.5
where the time goes:
time: 1110 us; the launch traced here: 1100 us
  waiting for transfers between devices  795 us (72%)
  blocking collectives  123 us (11%)
  matrix products  119 us (11%)
  other arithmetic  32.4 us (3%)
  between operations  14.5 us (1%)
  local copies, waits for them, and re-layouts  11.6 us (1%)
    psum x1, waiting for transfers between devices, per_device(): lax.psum(gate_local.astype(jnp.bfloat16), 'dp').astype(jnp.float32)  235 us
    reduce_scatter x1, waiting for transfers between devices, per_device(): lax.psum_scatter(in_local, ('dp', 'mp'), scatter_dimension=0, tiled=True)  158 us
    psum x1, waiting for transfers between devices, per_device(): lax.psum(jnp.dot(hidden, down_proj, preferred_element_type=jnp.float32).a...  134 us
    reduce_scatter x1, waiting for transfers between devices, per_device(): lax.psum_scatter(out_local, ('dp', 'mp'), scatter_dimension=0, tiled=True)  134 us
    unnamed x2, blocking collectives  82.6 us
    unnamed x10, waiting for transfers between devices  52 us
    dot_general x5, matrix products, inner_cols(): lax.dot_general(left, right, (((1,), (1,)), ((), ())), preferred_element_...  43.7 us
    all_gather x1, blocking collectives, per_device(): lax.all_gather(conv_kernel, ('dp', 'mp'), axis=0, tiled=True)  40.8 us
  transfers between devices with their start and end apart: 12, of which 10 were waited for; matrix products, arithmetic and copies ran while one was open for 9% of the time, Pallas kernels for 0%

commit v1 on v0

--- a/solution.py
+++ b/solution.py
@@ -132,7 +132,7 @@
     input_part, first_local = first_pull(first_grad)
     input_grad = (residual_grad + input_part).reshape(1, row_count, features)
     grad_gate, grad_up, grad_down = (
-        lax.psum(gate_local.astype(jnp.bfloat16), "dp").astype(jnp.float32),
+        jnp.sum(lax.all_gather(gate_local.astype(jnp.bfloat16), "dp"), axis=0).astype(jnp.float32),
         lax.psum(up_local.astype(jnp.bfloat16), "dp").astype(jnp.float32),
         lax.psum(down_local.astype(jnp.bfloat16), "dp").astype(jnp.float32),
     )

time: 1110 us -> 1410 us (1.27)
  waiting for transfers between devices: 795 us -> 1080 us
    all_gather x0 -> x1, waiting for transfers between devices: none -> 357 us  [per_device(): lax.all_gather(gate_local.astype(jnp.bfloat16), 'dp')]
    psum x1, waiting for transfers between devices: 235 us -> 169 us  [per_device(): lax.psum(up_local.astype(jnp.bfloat16), 'dp').astype(jnp.float32)]
    unnamed x10 -> x11, waiting for transfers between devices: 52 us -> 41.7 us
  transfers between devices with their start and end apart: 12 -> 13, of which waited for: 10 -> 11; matrix products, arithmetic and copies ran while one was open for 9% -> 8% of each run, Pallas kernels for 0% -> 0%
where the time goes in v1:
time: 1410 us; the launch traced here: 1400 us
  waiting for transfers between devices  1080 us (77%)
  blocking collectives  124 us (9%)
  matrix products  119 us (8%)
  other arithmetic  46 us (3%)
  between operations  14.8 us (1%)
    all_gather x1, waiting for transfers between devices, per_device(): lax.all_gather(gate_local.astype(jnp.bfloat16), 'dp')  357 us
    psum x1, waiting for transfers between devices, per_device(): lax.psum(up_local.astype(jnp.bfloat16), 'dp').astype(jnp.float32)  169 us
    reduce_scatter x1, waiting for transfers between devices, per_device(): lax.psum_scatter(in_local, ('dp', 'mp'), scatter_dimension=0, tiled=True)  159 us
    psum x1, waiting for transfers between devices, per_device(): lax.psum(jnp.dot(hidden, down_proj, preferred_element_type=jnp.float32).a...  143 us
    reduce_scatter x1, waiting for transfers between devices, per_device(): lax.psum_scatter(out_local, ('dp', 'mp'), scatter_dimension=0, tiled=True)  128 us
    unnamed x2, blocking collectives  83 us
    dot_general x5, matrix products, inner_cols(): lax.dot_general(left, right, (((1,), (1,)), ((), ())), preferred_element_...  43.7 us
    unnamed x11, waiting for transfers between devices  41.7 us
  transfers between devices with their start and end apart: 13, of which 11 were waited for; matrix products, arithmetic and copies ran while one was open for 8% of the time, Pallas kernels for 0%

profile of v1, /device:TPU:0, one launch (start us, length us, event | category | flops | bytes accessed | tf_op | source)
XLA Modules:
  0.0 1402.9 jit_solution(2486647343678046684)
XLA Ops:
  7.2 0.7 all-gather.9.cloned.1.call-update
  8.0 0.7 all-gather.11.cloned.1.call-update
  8.7 0.7 convert_element_type.91
  9.5 2.3 collective-permute-start
  11.9 0.8 dynamic-update-slice
  12.7 0.8 dynamic-update-slice.1
  13.5 41.9 %all-reduce.12 = (bf16[1024]{0:T(1024)(128)(2,1)S(1)}, bf16[1024]{0:T(1024)(128)(2,1)S(1)}) all-reduce(bf16[1024]{0:T(1024)(128)(2,1)S(1)} %dynamic-update-slice, bf16[1024]{0:T(1024)(128)(2,1)S(1)} %dynamic-update-slice.1), channel_id=1, replica_groups=mesh['dp'=8,'mp'=4] {'dp','mp'}, use_global_device_ids=true, to_apply=%add.7 | all-reduce | flops 2048 | bytes 8192
  55.4 40.6 %all-gather.2 = bf16[32,32,3]{1,2,0:T(4,128)(2,1)S(1)} all-gather(bf16[1,32,3]{1,2,0:T(4,128)(2,1)} %bitcast.76), channel_id=1, replica_groups=mesh['dp'=8,'mp'=4] {'dp','mp'}, dimensions={0}, use_global_device_ids=true | all-gather | bytes 6336 | tf_op jit(solution)/shard_map/all_gather | solution.py:70
  96.1 1.5 fusion.24
  97.7 6.0 fusion.35
  103.8 0.4 slice_multiply_fusion
  104.2 2.2 collective-permute-start.1
  106.5 0.7 collective-permute-done.1
  107.2 2.5 multiply_convert_fusion.6
  109.7 31.6 %all-gather.11.cloned.1.call-done = bf16[1024,1024]{1,0:T(8,128)(2,1)} async-done(((bf16[32,1024]{1,0:T(8,128)(2,1)}), bf16[1024,1024]{1,0:T(8,128)(2,1)}) %all-gather.11.cloned.1.call-update) | async-done | bytes 2097168 | tf_op jit(solution)/shard_map/all_gather | solution.py:71
  141.3 3.3 multiply_reduce_fusion.3
  144.6 1.4 copy-done.7
  146.0 1.2 multiply_convert_fusion.5
  147.2 0.5 all-gather.15.cloned.1.call-update
  147.8 0.6 all-reduce.20.cloned.1.call-start
  148.3 32.3 %all-gather.13.cloned.1.call-done = bf16[2048,1024]{1,0:T(8,128)(2,1)} async-done(((bf16[512,1024]{1,0:T(8,128)(2,1)}), bf16[2048,1024]{1,0:T(8,128)(2,1)}) %all-gather.13.cloned.1.call-update) | async-done | bytes 4194320 | tf_op jit(solution)/shard_map/all_gather | solution.py:95
  180.7 10.6 fusion.42
  191.3 7.9 fusion.43
  199.2 17.5 %all-gather.15.cloned.1.call-done = bf16[1,2048,1024]{2,1,0:T(8,128)(2,1)} async-done(((bf16[1,512,1024]{2,1,0:T(8,128)(2,1)}), bf16[1,2048,1024]{2,1,0:T(8,128)(2,1)}) %all-gather.15.cloned.1.call-update) | async-done | bytes 4194320 | tf_op jit(solution)/shard_map/all_gather | solution.py:107
  216.6 18.2 %multiply_convert_fusion = (bf16[2048,1152]{1,0:T(8,128)(2,1)}, bf16[2048,1152]{1,0:T(8,128)(2,1)}, bf16[2048,1152]{1,0:T(8,128)(2,1)}) fusion(f32[2048,1152]{1,0:T(8,128)} %fusion.42, f32[2048,1152]{1,0:T(8,128)} %fusion.43, bf16[1152,1024]{1,0:T(8,128)(2,1)S(1)} %copy-done, bf16[1,2048,1024]{2,1,0:T(8,128)(2,1)} %all-gather.15.cloned.1.call-done), kind=kOutput, calls=%fused_computation.4 | convolution fusion | flops 4869586944 | bytes 39583744 | tf_op jit(solution)/shard_map/dot_general | solution.py:31
  234.9 7.7 fusion.44
  242.6 7.1 convolution_convert_fusion.2
  249.7 7.7 add_convert_fusion
  257.5 10.0 convolution_convert_fusion
  267.5 143.3 %all-reduce.20.cloned.1.call-done = (bf16[2048,1024]{1,0:T(8,128)(2,1)}, bf16[2048,1024]{1,0:T(8,128)(2,1)}) async-done(((bf16[2048,1024]{1,0:T(8,128)(2,1)}, bf16[2048,1024]{1,0:T(8,128)(2,1)}), (bf16[2048,1024]{1,0:T(8,128)(2,1)}, bf16[2048,1024]{1,0:T(8,128)(2,1)})) %all-reduce.20.cloned.1.call-update) | async-done | bytes 8388624 | tf_op jit(solution)/shard_map/psum | solution.py:101
  410.8 2.0 fusion.20
  412.9 3.4 fusion.21
  416.3 1.3 fusion.32
  417.6 1.0 copy-done.4
  418.6 0.6 copy-done.10
  419.3 3.7 multiply_reduce_fusion.1
  423.0 1.1 copy.24
  424.1 9.3 fusion.8
  433.5 10.1 convolution_convert_fusion.1
  443.7 1.5 copy-done.6
  445.2 4.5 fusion.30
  449.8 2.0 multiply_select_fusion.2
  451.8 1.6 collective-permute-start.2
  453.4 1.0 pad_add_fusion
  454.4 0.8 collective-permute-done.2
  455.2 0.8 multiply_convert_fusion.4
  456.1 1.0 copy-done.12
  457.0 0.3 copy-done.13
  457.3 6.8 fusion.27
  464.2 8.8 fusion.18
  473.0 41.1 %all-reduce.11 = (f32[1024]{0:T(1024)S(1)}, f32[1024]{0:T(1024)S(1)}) all-reduce(f32[1024]{0:T(1024)S(1)} %get-tuple-element.15, f32[1024]{0:T(1024)S(1)} %get-tuple-element.10), channel_id=4, replica_groups=mesh['dp'=8,'mp'=4] {'dp','mp'}, use_global_device_ids=true, to_apply=%region_7.8.clone | all-reduce | flops 2048 | bytes 16384
  514.1 0.6 dynamic-slice
  514.7 0.6 dynamic-slice.1
  515.3 3.4 fusion.23
  518.7 39.7 %reduce-scatter.10.cloned.1.call-done = f32[32,3]{1,0:T(8,128)} async-done(((f32[1024,3]{1,0:T(8,128)}), f32[32,3]{1,0:T(8,128)}) %reduce-scatter.10.cloned.1.call-update) | async-done | bytes 400
  558.4 1.4 copy.25
  559.8 169.4 %all-reduce.18.cloned.1.call-done = (bf16[1024,1152]{1,0:T(8,128)(2,1)}, bf16[1152,1024]{1,0:T(8,128)(2,1)}) async-done(((bf16[1024,1152]{1,0:T(8,128)(2,1)}, bf16[1152,1024]{1,0:T(8,128)(2,1)}), (bf16[1024,1152]{1,0:T(8,128)(2,1)}, bf16[1152,1024]{1,0:T(8,128)(2,1)})) %all-reduce.18.cloned.1.call-update) | async-done | bytes 4718608 | tf_op jit(solution)/shard_map/psum | solution.py:136
  729.1 4.3 convert_element_type.110
  733.4 2.7 convert_element_type.112
  736.1 356.6 %all-gather.17.cloned.1.call-done = bf16[8192,1152]{1,0:T(8,128)(2,1)} async-done(((bf16[1024,1152]{1,0:T(8,128)(2,1)}), bf16[8192,1152]{1,0:T(8,128)(2,1)}) %all-gather.17.cloned.1.call-update) | async-done | bytes 18874384 | tf_op jit(solution)/shard_map/all_gather | solution.py:135
  1092.8 12.0 reduce_sum.107
  1104.8 4.2 convert_element_type.108
  1108.9 128.1 %reduce-scatter.8.cloned.1.call-done = f32[32,1024]{1,0:T(8,128)} async-done(((f32[1024,1024]{1,0:T(8,128)}), f32[32,1024]{1,0:T(8,128)}) %reduce-scatter.8.cloned.1.call-update) | async-done | bytes 131088 | tf_op jit(solution)/shard_map/reduce_scatter | solution.py:143
  1237.1 158.8 %reduce-scatter.6.cloned.1.call-done = f32[32,3072]{1,0:T(8,128)} async-done(((f32[1024,3072]{1,0:T(8,128)}), f32[32,3072]{1,0:T(8,128)}) %reduce-scatter.6.cloned.1.call-update) | async-done | bytes 393232 | tf_op jit(solution)/shard_map/reduce_scatter | solution.py:141
  (83 shorter events, 1.0 us)
Async XLA Ops:
  7.2 209.4 %copy-start = (bf16[1152,1024]{1,0:T(8,128)(2,1)S(1)}, bf16[1152,1024]{1,0:T(8,128)(2,1)}, u32[]{:S(2)}) copy-start(bf16[1152,1024]{1,0:T(8,128)(2,1)} %param.20) | copy-start | bytes 7077892
  7.2 90.5 %all-gather.9.cloned.1.call-start = ((), (), s32[]{:S(2)}) async-start(), calls=%async_computation.3 | async-start | bytes 6488064 | tf_op jit(solution)/shard_map/all_gather | solution.py:69
  7.9 133.4 %all-gather.11.cloned.1.call-start = ((), (), s32[]{:S(2)}) async-start(), calls=%async_computation.4 | async-start | bytes 2162688 | tf_op jit(solution)/shard_map/all_gather | solution.py:71
  8.7 172.0 %all-gather.13.cloned.1.call-start = ((), (), s32[]{:S(2)}) async-start(), calls=%async_computation.5 | async-start | bytes 5242880 | tf_op jit(solution)/shard_map/all_gather | solution.py:95
  9.5 88.2 %collective-permute-start = (f32[2]{0:T(128)S(1)}, f32[2]{0:T(128)S(1)}, u32[]{:S(2)}, u32[]{:S(2)}) collective-permute-start(f32[2]{0:T(128)S(1)} %slice_bitcast_fusion), channel_id=1, source_target_pairs={{0,1},{1,2},{2,3},{4,5},{5,6},{6,7},{8,9},{9,10},{10,11},{12,13},{... | collective-permute-start | bytes 32 | tf_op jit(solution)/shard_map/ppermute | solution.py:13
  103.8 3.5 copy-start.2
  104.2 3.1 copy-start.3
  104.2 3.0 collective-permute-start.1
  107.2 34.1 %copy-start.9 = (bf16[1,512,1024]{2,1,0:T(8,128)(2,1)S(1)}, bf16[1,512,1024]{2,1,0:T(8,128)(2,1)}, u32[]{:S(2)}) copy-start(bf16[1,512,1024]{2,1,0:T(8,128)(2,1)} %param.11) | copy-start | bytes 3145732
  144.6 1.4 copy-start.7
  147.2 69.4 %all-gather.15.cloned.1.call-start = ((), (), s32[]{:S(2)}) async-start(), calls=%async_computation.8 | async-start | bytes 5242880 | tf_op jit(solution)/shard_map/all_gather | solution.py:107
  147.8 263.1 %all-reduce.20.cloned.1.call-start = ((), (), s32[]{:S(2)}) async-start(), calls=%async_computation.12 | async-start | bytes 16777216 | tf_op jit(solution)/shard_map/psum | solution.py:101
  180.7 10.6 copy-start.16
  180.7 10.6 copy-start.18
  216.6 18.2 %copy-start.17 = (bf16[1024,1152]{1,0:T(8,128)(2,1)S(1)}, bf16[1024,1152]{1,0:T(8,128)(2,1)}, u32[]{:S(2)}) copy-start(bf16[1024,1152]{1,0:T(8,128)(2,1)} %param.18) | copy-start | bytes 7077892
  234.9 7.7 copy-start.21
  234.9 14.8 %slice-start.2 = ((s8[4718592]{0:T(1024)(128)(4,1)}), s8[4194304]{0:T(1024)(128)(4,1)S(1)}, s32[]{:S(2)}) async-start(s8[4718592]{0:T(1024)(128)(4,1)} %bitcast.77), calls=%async_computation.15 | async-start | bytes 8388608
  242.5 7.2 slice-start.3
  242.6 7.1 copy-start.19
  257.4 301.0 %reduce-scatter.10.cloned.1.call-start = ((), (), s32[]{:S(2)}) async-start(), calls=%async_computation.10 | async-start | bytes 540672
  257.5 153.3 %copy-start.8 = (f32[512,1024]{1,0:T(8,128)S(1)}, f32[512,1024]{1,0:T(8,128)}, u32[]{:S(2)}) copy-start(f32[512,1024]{1,0:T(8,128)} %copy-done.7) | copy-start | bytes 6291460
  410.8 2.0 copy-start.14
  412.9 3.4 copy-start.20
  416.3 1.3 copy-start.5
  416.3 2.3 copy-start.4
  416.3 3.0 copy-start.10
  424.0 305.1 %all-reduce.18.cloned.1.call-start = ((), (), s32[]{:S(2)}) async-start(), calls=%async_computation.11 | async-start | bytes 9437184 | tf_op jit(solution)/shard_map/psum | solution.py:136
  433.4 659.3 %all-gather.17.cloned.1.call-start = ((), (), s32[]{:S(2)}) async-start(), calls=%async_computation.9 | async-start | bytes 21233664 | tf_op jit(solution)/shard_map/all_gather | solution.py:135
  443.6 1.6 copy-start.6
  443.6 793.4 %reduce-scatter.8.cloned.1.call-start = ((), (), s32[]{:S(2)}) async-start(), calls=%async_computation.7 | async-start | bytes 4325376 | tf_op jit(solution)/shard_map/reduce_scatter | solution.py:143
  449.7 946.1 %reduce-scatter.6.cloned.1.call-start = ((), (), s32[]{:S(2)}) async-start(), calls=%async_computation.6 | async-start | bytes 12976128 | tf_op jit(solution)/shard_map/reduce_scatter | solution.py:141
  451.8 3.4 slice-start
  451.8 3.3 slice-start.1
  451.8 3.3 collective-permute-start.2
  454.4 3.0 copy-start.11
  456.0 1.0 copy-start.12
  456.0 1.3 copy-start.13
  729.1 4.3 copy-start.15
  1092.8 303.0 %copy-start.1 = (bf16[1152,1024]{1,0:T(8,128)(2,1)S(1)}, bf16[1152,1024]{1,0:T(8,128)(2,1)}, u32[]{:S(2)}) copy-start(bf16[1152,1024]{1,0:T(8,128)(2,1)} %param.20) | copy-start | bytes 7077892
Sparse Core Ops, SparseCore 0:
  10.9 72.5 all-gather.8
  86.4 54.8 all-gather.10
  147.3 33.3 all-gather.12
  182.1 34.4 all-gather.14
  257.6 153.2 all-reduce.19
  424.2 134.1 reduce-scatter.9
  563.0 166.0 all-reduce.17
  731.3 361.4 all-gather.16
  1095.7 141.2 reduce-scatter.7
  1244.5 151.2 reduce-scatter.5
